TPU v7x, 128 devices: a whole 4x4x4 slice. The times are simulated.
128 devices in a mesh: seq: 16 (over y_lo, x, core), cb: 8 (over y_hi, z).
Axes of the slice: x: 4, y: 4 (y_hi: 2, y_lo: 2; y = y_hi * 2 + y_lo), z: 4, core: 2. Of those that a mesh axis runs over, the one named last changes fastest.
Arguments:
- hidden: bfloat16 [2, 2048, 4096], P(None, 'seq'), may hold values from -6 to 6
- temporal_gain: float32 [4096], replicated, may hold values from 0.5 to 2
- temporal_qkv: bfloat16 [3, 4096, 2048], P(None, None, 'cb'), may hold values from -10 to 10
- temporal_out: bfloat16 [2048, 4096], P('cb'), may hold values from -0.125 to 0.125
- codebook_ids: int32 [2, 2048, 8], P(None, 'seq', 'cb'), may hold values from 0 to 2047
- embedding: bfloat16 [8, 2048, 1024], P('cb'), may hold values from -6 to 6
- input_weight: bfloat16 [8, 4096, 1024], P('cb', 'seq'), may hold values from -0.09375 to 0.09375
- depth_gain: float32 [8, 1024], P('cb'), may hold values from 0.5 to 2
- depth_qkv: bfloat16 [8, 3, 1024, 1024], P('cb'), may hold values from -10 to 10
- depth_out: bfloat16 [8, 1024, 1024], P('cb'), may hold values from -0.1875 to 0.1875
Outputs:
- temporal: bfloat16 [2, 2048, 4096], P(None, 'seq')
- depth: bfloat16 [2, 2048, 8, 1024], P(None, 'seq', 'cb')
All inputs are finite; a program needn't handle non-finite values.
Results may differ from a plain program's by a relative error of at most 0.017.
Values may be sent and summed in bfloat16 or wider, within the bound.
A program may use at most 128 MiB of HBM per device.

v0:
```python
import jax
import jax.numpy as jnp
from jax import lax
from jax.sharding import PartitionSpec as P

HD = 128
DW = 1024
DH = 16
DHD = 64


def normalize(values, scale):
    mean_sq = jnp.mean(values * values, axis=-1, keepdims=True)
    return values * lax.rsqrt(mean_sq + 1e-05) * scale


def shards(
    hidden,
    temporal_gain,
    temporal_qkv,
    temporal_out,
    codebook_ids,
    embedding,
    input_weight,
    depth_gain,
    depth_qkv,
    depth_out,
):
    seq_count, frames, width = hidden.shape
    head_cols = temporal_qkv.shape[2]
    head_count = head_cols // HD
    row_count = seq_count * frames
    hidden_f = hidden.astype(jnp.float32)
    normed = normalize(hidden_f, temporal_gain).astype(jnp.bfloat16).reshape(row_count, width)
    projected = []
    for which in range(3):
        part_rows = jnp.dot(normed, temporal_qkv[which], preferred_element_type=jnp.float32).astype(
            jnp.bfloat16
        )
        projected.append(part_rows.reshape(seq_count, frames, head_count, HD))
    queries = projected[0]
    query_pos = lax.axis_index("seq") * frames + jnp.arange(frames, dtype=jnp.int32)
    temporal_scale = 1.0 / jnp.sqrt(jnp.float32(HD))
    highest = jnp.full((seq_count, head_count, frames), -1e30, jnp.float32)
    key_piece = lax.all_gather(projected[1], "seq", axis=1, tiled=True)
    value_piece = lax.all_gather(projected[2], "seq", axis=1, tiled=True)
    count = key_piece.shape[1]
    scores = (
        jnp.einsum("sqhd,skhd->shqk", queries, key_piece, preferred_element_type=jnp.float32)
        * temporal_scale
    )
    key_pos = jnp.arange(count, dtype=jnp.int32)
    allowed = (key_pos[None, :] <= query_pos[:, None])[None, None]
    scores = jnp.where(allowed, scores, -1e30)
    new_high = jnp.maximum(highest, jnp.max(scores, axis=-1))
    weights = jnp.where(allowed, jnp.exp(scores - new_high[..., None]), 0.0)
    totals = jnp.sum(weights, axis=-1)
    update = jnp.einsum(
        "shqk,skhd->sqhd",
        weights.astype(jnp.bfloat16),
        value_piece,
        preferred_element_type=jnp.float32,
    )
    gathered = update
    highest, totals, gathered = (new_high, totals, gathered)
    mixed = (
        (gathered / totals.transpose(0, 2, 1)[..., None])
        .astype(jnp.bfloat16)
        .reshape(row_count, head_cols)
    )
    term = jnp.dot(mixed, temporal_out, preferred_element_type=jnp.float32)
    summed = lax.psum(term.astype(jnp.bfloat16), "cb").astype(jnp.float32)
    temporal = (hidden_f.reshape(row_count, width) + summed).astype(jnp.bfloat16)
    projected_in = jnp.dot(
        temporal,
        lax.all_gather(input_weight, "seq", axis=1, tiled=True)[0],
        preferred_element_type=jnp.float32,
    )
    entry = jnp.take(embedding[0], codebook_ids.reshape(row_count), axis=0).astype(jnp.float32)
    stream = (projected_in + entry).astype(jnp.bfloat16)
    depth_normed = normalize(stream.astype(jnp.float32), depth_gain[0]).astype(jnp.bfloat16)
    book_query = jnp.dot(depth_normed, depth_qkv[0, 0], preferred_element_type=jnp.float32).astype(
        jnp.bfloat16
    )
    book_key = jnp.dot(depth_normed, depth_qkv[0, 1], preferred_element_type=jnp.float32).astype(
        jnp.bfloat16
    )
    book_value = jnp.dot(depth_normed, depth_qkv[0, 2], preferred_element_type=jnp.float32).astype(
        jnp.bfloat16
    )
    depth_scale = 1.0 / jnp.sqrt(jnp.float32(DHD))
    my_book = lax.axis_index("cb")
    query_heads = book_query.reshape(row_count, DH, DHD)
    highest_b = jnp.full((row_count, DH), -1e30, jnp.float32)
    key_piece = lax.all_gather(book_key[None], "cb", axis=0, tiled=True)
    value_piece = lax.all_gather(book_value[None], "cb", axis=0, tiled=True)
    count = key_piece.shape[0]
    key_heads = key_piece.reshape(count, row_count, DH, DHD)
    value_heads = value_piece.reshape(count, row_count, DH, DHD)
    scores = (
        jnp.einsum("rhd,jrhd->rhj", query_heads, key_heads, preferred_element_type=jnp.float32)
        * depth_scale
    )
    permitted = (jnp.arange(count, dtype=jnp.int32) <= my_book)[None, None, :]
    scores = jnp.where(permitted, scores, -1e30)
    new_high = jnp.maximum(highest_b, jnp.max(scores, axis=-1))
    weights = jnp.where(permitted, jnp.exp(scores - new_high[..., None]), 0.0)
    totals_b = jnp.sum(weights, axis=-1)
    update = jnp.einsum(
        "rhj,jrhd->rhd",
        weights.astype(jnp.bfloat16),
        value_heads,
        preferred_element_type=jnp.float32,
    )
    highest_b, totals_b, gathered_b = (new_high, totals_b, update)
    book_mixed = (gathered_b / totals_b[..., None]).astype(jnp.bfloat16).reshape(row_count, DW)
    depth = (
        jnp.dot(book_mixed, depth_out[0], preferred_element_type=jnp.float32)
        + stream.astype(jnp.float32)
    ).astype(jnp.bfloat16)
    return (temporal.reshape(seq_count, frames, width), depth.reshape(seq_count, frames, 1, DW))


def solution(mesh):
    placed = (
        P(None, "seq", None),
        P(),
        P(None, None, "cb"),
        P("cb", None),
        P(None, "seq", "cb"),
        P("cb", None, None),
        P("cb", "seq", None),
        P("cb", None),
        P("cb", None, None, None),
        P("cb", None, None),
    )
    return jax.shard_map(
        shards,
        mesh=mesh,
        in_specs=placed,
        out_specs=(P(None, "seq", None), P(None, "seq", "cb", None)),
        check_vma=False,
    )
```

profile of v0, /device:TPU:1, one launch (start us, length us, event | category | flops | bytes accessed | tf_op | source)
XLA Modules:
  0.0 419.6 jit_solution(1029900267491474171)
XLA Ops:
  7.2 2.2 multiply_reduce_fusion.2
  9.5 2.3 multiply_convert_fusion
  11.8 1.3 copy-done.5
  13.1 2.3 fusion.58
  15.5 0.7 copy.25
  16.3 2.9 fusion.52
  19.2 0.8 copy.24
  20.1 2.9 fusion.55
  23.3 30.6 %all-gather.10.cloned.1.call-done = bf16[2,2048,2,128]{3,1,2,0:T(8,128)(2,1)} async-done(((bf16[2,128,2,128]{3,1,2,0:T(8,128)(2,1)}), bf16[2,2048,2,128]{3,1,2,0:T(8,128)(2,1)}) %all-gather.10.cloned.1.call-update) | async-done | bytes 2097168 | tf_op jit(solution)/shard_map/all_gather | solution.py:45
  53.9 2.6 fusion.3
  56.6 1.9 copy-done.3
  58.5 1.3 fusion.4
  59.7 33.6 %all-gather.8.cloned.1.call-done = bf16[2,2048,2,128]{1,3,2,0:T(8,128)(2,1)} async-done(((bf16[2,128,2,128]{1,3,2,0:T(8,128)(2,1)}), bf16[2,2048,2,128]{1,3,2,0:T(8,128)(2,1)}) %all-gather.8.cloned.1.call-update) | async-done | bytes 2097168 | tf_op jit(solution)/shard_map/all_gather | solution.py:46
  93.4 4.1 fusion.64
  97.6 2.0 convolution_convert_fusion
  100.6 4.3 %gather_fusion = bf16[256,1024]{1,0:T(8,128)(2,1)S(1)} fusion(bf16[2048,1024]{1,0:T(8,128)(2,1)} %bitcast.102, s32[1024]{0:T(1024)S(1)} %pad_clamp_fusion), kind=kCustom, calls=%fused_computation | custom fusion | bytes 1049600 | tf_op jit(solution)/shard_map/jit(_take)/gather | solution.py:79
  104.9 82.8 %all-reduce.2.cloned.1.call-done = bf16[256,4096]{1,0:T(8,128)(2,1)} async-done(((bf16[256,4096]{1,0:T(8,128)(2,1)}), bf16[256,4096]{1,0:T(8,128)(2,1)}) %all-reduce.2.cloned.1.call-update) | async-done | bytes 2097168 | tf_op jit(solution)/shard_map/psum | solution.py:72
  187.7 3.7 fusion.2
  191.4 53.9 %all-gather.12.cloned.1.call-done = bf16[1,4096,1024]{2,1,0:T(8,128)(2,1)} async-done(((bf16[1,256,1024]{2,1,0:T(8,128)(2,1)}), bf16[1,4096,1024]{2,1,0:T(8,128)(2,1)}) %all-gather.12.cloned.1.call-update) | async-done | bytes 8388624 | tf_op jit(solution)/shard_map/all_gather | solution.py:76
  245.2 6.5 %fusion.67 = (f32[256]{0:T(256)S(1)}, bf16[256,1024]{1,0:T(8,128)(2,1)S(1)}) fusion(bf16[256,1024]{1,0:T(8,128)(2,1)S(1)} %gather_fusion, pred[256]{0:T(512)(128)(4,1)S(1)} %compare_and_fusion, bf16[256,4096]{1,0:T(8,128)(2,1)} %fusion.2, bf16[1,4096,1024]{2,1,0:T(8,128)(2,1)} %all-gather.12.cloned.1.call-done), kind=kOutput, calls=%fused_computation.52 | convolution fusion | flops 2149318400 | bytes 11535616 | tf_op jit(solution)/shard_map/dot_general | solution.py:74
  251.7 3.1 fusion.43
  255.1 3.2 fusion.46
  258.4 2.4 fusion.40
  261.1 65.6 %all-gather.14.cloned.1.call-done = bf16[2048,1024]{1,0:T(8,128)(2,1)} async-done(((bf16[256,1024]{1,0:T(8,128)(2,1)}), bf16[2048,1024]{1,0:T(8,128)(2,1)}) %all-gather.14.cloned.1.call-update) | async-done | bytes 4194320 | tf_op jit(solution)/shard_map/all_gather | solution.py:95
  326.7 6.5 %copy.29 = bf16[2048,1024]{0,1:T(8,128)(2,1)} copy(bf16[2048,1024]{1,0:T(8,128)(2,1)} %all-gather.14.cloned.1.call-done) | data formatting | bytes 8388608 | tf_op jit(solution)/shard_map/all_gather | solution.py:95
  333.1 3.7 copy.47
  336.8 0.9 multiply_reduce_fusion.1
  338.0 60.2 %all-gather.16.cloned.1.call-done = bf16[2048,1024]{1,0:T(8,128)(2,1)} async-done(((bf16[256,1024]{1,0:T(8,128)(2,1)}), bf16[2048,1024]{1,0:T(8,128)(2,1)}) %all-gather.16.cloned.1.call-update) | async-done | bytes 4194320 | tf_op jit(solution)/shard_map/all_gather | solution.py:96
  398.2 6.5 %copy.30 = bf16[2048,1024]{0,1:T(8,128)(2,1)} copy(bf16[2048,1024]{1,0:T(8,128)(2,1)} %all-gather.16.cloned.1.call-done) | data formatting | bytes 8388608 | tf_op jit(solution)/shard_map/all_gather | solution.py:96
  404.7 3.7 copy.48
  408.4 2.6 multiply_reduce_fusion
  411.2 1.5 fusion.37
  (45 shorter events, 2.5 us)
Async XLA Ops:
  7.2 90.5 %copy-start = (bf16[256,4096]{1,0:T(8,128)(2,1)S(1)}, bf16[256,4096]{1,0:T(8,128)(2,1)}, u32[]{:S(2)}) copy-start(bf16[256,4096]{1,0:T(8,128)(2,1)} %param.13) | copy-start | bytes 6291460
  7.2 46.7 %all-gather.10.cloned.1.call-start = ((), (), s32[]{:S(2)}) async-start(), calls=%async_computation.1 | async-start | bytes 2228224 | tf_op jit(solution)/shard_map/all_gather | solution.py:45
  11.8 1.3 copy-start.5
  16.2 77.2 %all-gather.8.cloned.1.call-start = ((), (), s32[]{:S(2)}) async-start(), calls=%async_computation | async-start | bytes 2228224 | tf_op jit(solution)/shard_map/all_gather | solution.py:46
  20.0 167.7 %all-reduce.2.cloned.1.call-start = ((), (), s32[]{:S(2)}) async-start(), calls=%async_computation.2 | async-start | bytes 4194304 | tf_op jit(solution)/shard_map/psum | solution.py:72
  56.5 1.9 copy-start.3
  97.5 3.0 copy-start.6
  99.7 88.0 %copy-start.2 = (bf16[2,128,4096]{2,1,0:T(8,128)(2,1)S(1)}, bf16[2,128,4096]{2,1,0:T(8,128)(2,1)}, u32[]{:S(2)}) copy-start(bf16[2,128,4096]{2,1,0:T(8,128)(2,1)} %param.10) | copy-start | bytes 6291460
  99.7 145.5 %all-gather.12.cloned.1.call-start = ((), (), s32[]{:S(2)}) async-start(), calls=%async_computation.3 | async-start | bytes 8912896 | tf_op jit(solution)/shard_map/all_gather | solution.py:76
  100.3 226.4 %all-gather.14.cloned.1.call-start = ((), (), s32[]{:S(2)}) async-start(), calls=%async_computation.4 | async-start | bytes 4718592 | tf_op jit(solution)/shard_map/all_gather | solution.py:95
  191.4 60.3 %copy-start.7 = (f32[1,1024]{1,0:T(1,128)S(1)}, f32[1,1024]{1,0:T(1,128)}, u32[]{:S(2)}) copy-start(f32[1,1024]{1,0:T(1,128)} %param.17) | copy-start | bytes 12292
  254.9 143.3 %all-gather.16.cloned.1.call-start = ((), (), s32[]{:S(2)}) async-start(), calls=%async_computation.5 | async-start | bytes 4718592 | tf_op jit(solution)/shard_map/all_gather | solution.py:96
  408.4 2.8 copy-start.4
  408.4 4.3 %copy-start.1 = (bf16[256,4096]{1,0:T(8,128)(2,1)S(1)}, bf16[256,4096]{1,0:T(8,128)(2,1)}, u32[]{:S(2)}) copy-start(bf16[256,4096]{1,0:T(8,128)(2,1)} %param.13) | copy-start | bytes 6291460
Sparse Core Ops, SparseCore 0:
  16.3 37.5 all-gather.9
  56.1 37.2 all-gather.7
  99.8 87.8 all-reduce.1
  189.2 55.9 all-gather.11
  255.0 71.6 all-gather.13
  328.9 69.2 all-gather.15
where the time goes:
time: 420 us
  waiting for transfers between devices  327 us (78%)
  matrix products  33.6 us (8%)
  local copies, waits for them, and re-layouts  29.8 us (7%)
  between operations  14.4 us (3%)
  other arithmetic  13.8 us (3%)
    psum x1, waiting for transfers between devices, shards(): summed = lax.psum(term.astype(jnp.bfloat16), 'cb').astype(jnp.float32)  82.8 us
    all_gather x1, waiting for transfers between devices, shards(): key_piece = lax.all_gather(book_key[None], 'cb', axis=0, tiled=True)  65.6 us
    all_gather x1, waiting for transfers between devices, shards(): value_piece = lax.all_gather(book_value[None], 'cb', axis=0, tiled=True)  60.2 us
    all_gather x1, waiting for transfers between devices, shards(): lax.all_gather(input_weight, 'seq', axis=1, tiled=True)[0]  53.9 us
    all_gather x1, waiting for transfers between devices, shards(): value_piece = lax.all_gather(projected[2], 'seq', axis=1, tiled=True)  33.6 us
    all_gather x1, waiting for transfers between devices, shards(): key_piece = lax.all_gather(projected[1], 'seq', axis=1, tiled=True)  30.6 us
    unnamed x18, local copies, waits for them, and re-layouts  10.6 us
  transfers between devices with their start and end apart: 6, of which 6 were waited for; matrix products, arithmetic and copies ran while one was open for 9% of the time, Pallas kernels for 0%

commit v1 on v0

--- a/solution.py
+++ b/solution.py
@@ -69,7 +69,7 @@
         .reshape(row_count, head_cols)
     )
     term = jnp.dot(mixed, temporal_out, preferred_element_type=jnp.float32)
-    summed = lax.psum(term.astype(jnp.bfloat16), "cb").astype(jnp.float32)
+    summed = jnp.sum(lax.all_gather(term.astype(jnp.bfloat16), "cb"), axis=0).astype(jnp.float32)
     temporal = (hidden_f.reshape(row_count, width) + summed).astype(jnp.bfloat16)
     projected_in = jnp.dot(
         temporal,

time: 420 us -> 509 us (1.21)
  waiting for transfers between devices: 327 us -> 406 us
  other arithmetic: 13.8 us -> 24.3 us
    all_gather x0 -> x1, waiting for transfers between devices: none -> 177 us  [shards(): lax.all_gather(term.astype(jnp.bfloat16), 'cb')]
    psum x1 -> x0, waiting for transfers between devices: 82.8 us -> none  [shards(): summed = lax.psum(term.astype(jnp.bfloat16), 'cb').astype(jnp.float32)]
    all_gather x1, waiting for transfers between devices: 53.9 us -> 37.9 us  [shards(): lax.all_gather(input_weight, 'seq', axis=1, tiled=True)[0]]
    reduce_sum x0 -> x1, other arithmetic: none -> 10.6 us  [shards(): jnp.sum(lax.all_gather(term.astype(jnp.bfloat16), 'cb'), axis=0)]
where the time goes in v1:
time: 509 us
  waiting for transfers between devices  406 us (80%)
  matrix products  33.6 us (7%)
  local copies, waits for them, and re-layouts  29.8 us (6%)
  other arithmetic  24.3 us (5%)
  between operations  14.4 us (3%)
    all_gather x1, waiting for transfers between devices, shards(): lax.all_gather(term.astype(jnp.bfloat16), 'cb')  177 us
    all_gather x1, waiting for transfers between devices, shards(): key_piece = lax.all_gather(book_key[None], 'cb', axis=0, tiled=True)  65.6 us
    all_gather x1, waiting for transfers between devices, shards(): value_piece = lax.all_gather(book_value[None], 'cb', axis=0, tiled=True)  60.2 us
    all_gather x1, waiting for transfers between devices, shards(): lax.all_gather(input_weight, 'seq', axis=1, tiled=True)[0]  37.9 us
    all_gather x1, waiting for transfers between devices, shards(): value_piece = lax.all_gather(projected[2], 'seq', axis=1, tiled=True)  33.6 us
    all_gather x1, waiting for transfers between devices, shards(): key_piece = lax.all_gather(projected[1], 'seq', axis=1, tiled=True)  30.6 us
    unnamed x18, local copies, waits for them, and re-layouts  10.6 us
    reduce_sum x1, other arithmetic, shards(): jnp.sum(lax.all_gather(term.astype(jnp.bfloat16), 'cb'), axis=0)  10.6 us
  transfers between devices with their start and end apart: 6, of which 6 were waited for; matrix products, arithmetic and copies ran while one was open for 9% of the time, Pallas kernels for 0%

profile of v1, /device:TPU:1, one launch (start us, length us, event | category | flops | bytes accessed | tf_op | source)
XLA Modules:
  0.0 508.6 jit_solution(13797044585109742676)
XLA Ops:
  7.2 2.2 fusion.2
  9.5 2.2 fusion.4
  11.7 1.3 copy-done.5
  13.0 2.3 fusion.61
  16.1 2.9 fusion.55
  19.1 0.8 copy.24
  20.0 2.9 fusion.58
  23.2 30.6 %all-gather.12.cloned.1.call-done = bf16[2,2048,2,128]{3,1,2,0:T(8,128)(2,1)} async-done(((bf16[2,128,2,128]{3,1,2,0:T(8,128)(2,1)}), bf16[2,2048,2,128]{3,1,2,0:T(8,128)(2,1)}) %all-gather.12.cloned.1.call-update) | async-done | bytes 2097168 | tf_op jit(solution)/shard_map/all_gather | solution.py:45
  53.8 2.6 fusion.6
  56.4 1.9 copy-done.3
  58.4 1.3 fusion.7
  59.6 33.6 %all-gather.10.cloned.1.call-done = bf16[2,2048,2,128]{1,3,2,0:T(8,128)(2,1)} async-done(((bf16[2,128,2,128]{1,3,2,0:T(8,128)(2,1)}), bf16[2,2048,2,128]{1,3,2,0:T(8,128)(2,1)}) %all-gather.10.cloned.1.call-update) | async-done | bytes 2097168 | tf_op jit(solution)/shard_map/all_gather | solution.py:46
  93.3 4.1 fusion.67
  97.5 2.0 convolution_convert_fusion
  100.4 4.3 gather_fusion
  104.7 177.3 %all-gather.16.cloned.1.call-done = bf16[2048,4096]{1,0:T(8,128)(2,1)} async-done(((bf16[256,4096]{1,0:T(8,128)(2,1)}), bf16[2048,4096]{1,0:T(8,128)(2,1)}) %all-gather.16.cloned.1.call-update) | async-done | bytes 16777232 | tf_op jit(solution)/shard_map/all_gather | solution.py:72
  282.0 10.6 %reduce_sum.50 = bf16[256,4096]{1,0:T(8,128)(2,1)} reduce(bf16[8,256,4096]{2,1,0:T(8,128)(2,1)} %bitcast.97, bf16[]{:T(256)} %constant.42.clone.1), dimensions={0}, to_apply=%region_3.4 | reduce | flops 7340032 | bytes 18874370 | tf_op jit(solution)/shard_map/reduce_sum | solution.py:72
  292.6 3.7 fusion.5
  296.3 37.9 %all-gather.14.cloned.1.call-done = bf16[1,4096,1024]{2,1,0:T(8,128)(2,1)} async-done(((bf16[1,256,1024]{2,1,0:T(8,128)(2,1)}), bf16[1,4096,1024]{2,1,0:T(8,128)(2,1)}) %all-gather.14.cloned.1.call-update) | async-done | bytes 8388624 | tf_op jit(solution)/shard_map/all_gather | solution.py:76
  334.2 6.5 %fusion.70 = (f32[256]{0:T(256)S(1)}, bf16[256,1024]{1,0:T(8,128)(2,1)S(1)}) fusion(bf16[256,1024]{1,0:T(8,128)(2,1)S(1)} %gather_fusion, pred[256]{0:T(512)(128)(4,1)S(1)} %compare_and_fusion, bf16[256,4096]{1,0:T(8,128)(2,1)} %bitcast.104, bf16[1,4096,1024]{2,1,0:T(8,128)(2,1)} %all-gather.14.cloned.1.call-done), kind=kOutput, calls=%fused_computation.55 | convolution fusion | flops 2149318400 | bytes 11535616 | tf_op jit(solution)/shard_map/dot_general | solution.py:74
  340.7 3.2 fusion.46
  344.2 3.2 fusion.49
  347.4 2.3 fusion.43
  350.0 65.6 %all-gather.18.cloned.1.call-done = bf16[2048,1024]{1,0:T(8,128)(2,1)} async-done(((bf16[256,1024]{1,0:T(8,128)(2,1)}), bf16[2048,1024]{1,0:T(8,128)(2,1)}) %all-gather.18.cloned.1.call-update) | async-done | bytes 4194320 | tf_op jit(solution)/shard_map/all_gather | solution.py:95
  415.7 6.5 %copy.29 = bf16[2048,1024]{0,1:T(8,128)(2,1)} copy(bf16[2048,1024]{1,0:T(8,128)(2,1)} %all-gather.18.cloned.1.call-done) | data formatting | bytes 8388608 | tf_op jit(solution)/shard_map/all_gather | solution.py:95
  422.1 3.7 copy.47
  425.8 0.9 multiply_reduce_fusion.1
  427.0 60.2 %all-gather.20.cloned.1.call-done = bf16[2048,1024]{1,0:T(8,128)(2,1)} async-done(((bf16[256,1024]{1,0:T(8,128)(2,1)}), bf16[2048,1024]{1,0:T(8,128)(2,1)}) %all-gather.20.cloned.1.call-update) | async-done | bytes 4194320 | tf_op jit(solution)/shard_map/all_gather | solution.py:96
  487.2 6.5 %copy.30 = bf16[2048,1024]{0,1:T(8,128)(2,1)} copy(bf16[2048,1024]{1,0:T(8,128)(2,1)} %all-gather.20.cloned.1.call-done) | data formatting | bytes 8388608 | tf_op jit(solution)/shard_map/all_gather | solution.py:96
  493.7 3.7 copy.48
  497.4 2.6 multiply_reduce_fusion
  500.2 1.5 fusion.40
  (46 shorter events, 3.1 us)
Async XLA Ops:
  7.2 90.4 %copy-start = (bf16[256,4096]{1,0:T(8,128)(2,1)S(1)}, bf16[256,4096]{1,0:T(8,128)(2,1)}, u32[]{:S(2)}) copy-start(bf16[256,4096]{1,0:T(8,128)(2,1)} %param.13) | copy-start | bytes 6291460
  7.2 46.6 %all-gather.12.cloned.1.call-start = ((), (), s32[]{:S(2)}) async-start(), calls=%async_computation.1 | async-start | bytes 2228224 | tf_op jit(solution)/shard_map/all_gather | solution.py:45
  11.7 1.3 copy-start.5
  16.1 77.2 %all-gather.10.cloned.1.call-start = ((), (), s32[]{:S(2)}) async-start(), calls=%async_computation | async-start | bytes 2228224 | tf_op jit(solution)/shard_map/all_gather | solution.py:46
  19.9 262.1 %all-gather.16.cloned.1.call-start = ((), (), s32[]{:S(2)}) async-start(), calls=%async_computation.3 | async-start | bytes 18874368 | tf_op jit(solution)/shard_map/all_gather | solution.py:72
  56.4 1.9 copy-start.3
  97.4 3.0 copy-start.6
  99.6 234.6 %all-gather.14.cloned.1.call-start = ((), (), s32[]{:S(2)}) async-start(), calls=%async_computation.2 | async-start | bytes 8912896 | tf_op jit(solution)/shard_map/all_gather | solution.py:76
  100.2 315.5 %all-gather.18.cloned.1.call-start = ((), (), s32[]{:S(2)}) async-start(), calls=%async_computation.4 | async-start | bytes 4718592 | tf_op jit(solution)/shard_map/all_gather | solution.py:95
  282.0 10.6 %copy-start.2 = (bf16[2,128,4096]{2,1,0:T(8,128)(2,1)S(1)}, bf16[2,128,4096]{2,1,0:T(8,128)(2,1)}, u32[]{:S(2)}) copy-start(bf16[2,128,4096]{2,1,0:T(8,128)(2,1)} %param.10) | copy-start | bytes 6291460
  334.2 6.5 %copy-start.7 = (f32[1,1024]{1,0:T(1,128)S(1)}, f32[1,1024]{1,0:T(1,128)}, u32[]{:S(2)}) copy-start(f32[1,1024]{1,0:T(1,128)} %param.17) | copy-start | bytes 12292
  343.9 143.3 %all-gather.20.cloned.1.call-start = ((), (), s32[]{:S(2)}) async-start(), calls=%async_computation.5 | async-start | bytes 4718592 | tf_op jit(solution)/shard_map/all_gather | solution.py:96
  497.4 2.8 copy-start.4
  497.4 4.3 copy-start.1
Sparse Core Ops, SparseCore 0:
  16.2 37.5 all-gather.11
  56.0 37.2 all-gather.9
  99.7 182.2 all-gather.15
  283.6 50.6 all-gather.13
  344.0 71.6 all-gather.17
  417.9 69.2 all-gather.19
